TPU v7x, 32 devices: a whole 2x2x4 slice. The times are simulated.
32 devices in a mesh: dp: 4 (over x, core), mp: 8 (over z, y).
Axes of the slice: x: 2, y: 2, z: 4, core: 2. Of those that a mesh axis runs over, the one named last changes fastest.
Arguments:
- hidden: bfloat16 [4, 4, 512, 2048], P('dp', None, None, 'mp'), may hold values from -6 to 6
- gain: float32 [2048], P('mp'), may hold values from 0.1 to 1.9
- cotangent: bfloat16 [4, 4, 512, 2048], P('dp', None, None, 'mp'), may hold values from -600 to 600
- blocks: int32 [4, 4, 2], P('dp'), may hold values from 1 to 2
- loss_mask: int32 [4, 4, 512], P('dp'), may hold values 0 or 1
- wi_gate: bfloat16 [5120, 2048], P('mp'), may hold values from -0.125 to 0.125
- wi_up: bfloat16 [5120, 2048], P('mp'), may hold values from -0.125 to 0.125
- wo_weight: bfloat16 [5120, 2048], P('mp'), may hold values from -0.078125 to 0.078125
Outputs:
- gradients: float32 [3, 5120, 2048], P(None, 'mp')
Inputs may be any that keep to these rules, and one draw needn't show every extreme that they name: blocks of 128 target positions used by a sequence; later positions are padding.
All inputs are finite; a program needn't handle non-finite values. No bound on the sum of `loss_mask` on one device may be relied on, other than what follows from the above.
Results may differ from a plain program's by a relative error of at most 0.0059.
Values may be sent and summed in bfloat16 or wider, within the bound.
A program may use at most 128 MiB of HBM per device.

v0:
```python
import jax
import jax.numpy as jnp
from jax import lax
from jax.sharding import PartitionSpec as P

D = 2048
BLOCK = 128
TLEN = 256


def gelu_tanh(value):
    return jax.nn.gelu(value, approximate=True)


def contributions(normed, tangent, wi_gate, wi_up, wo_weight):
    rows_dims = (((1,), (1,)), ((), ()))
    gate_pre = lax.dot_general(normed, wi_gate, rows_dims, preferred_element_type=jnp.float32)
    up_pre = lax.dot_general(normed, wi_up, rows_dims, preferred_element_type=jnp.float32)
    activated, pullback = jax.vjp(gelu_tanh, gate_pre)
    inner = (activated * up_pre).astype(jnp.bfloat16)
    back_grad = lax.dot_general(tangent, wo_weight, rows_dims, preferred_element_type=jnp.float32)
    grad_gate = pullback(back_grad * up_pre)[0].astype(jnp.bfloat16)
    grad_up = (back_grad * activated).astype(jnp.bfloat16)
    dims = (((0,), (0,)), ((), ()))
    first_grad = lax.dot_general(grad_gate, normed, dims, preferred_element_type=jnp.float32)
    second_grad = lax.dot_general(grad_up, normed, dims, preferred_element_type=jnp.float32)
    third_grad = lax.dot_general(inner, tangent, dims, preferred_element_type=jnp.float32)
    return jnp.stack([first_grad, second_grad, third_grad])


def on_device(hidden, gain, cotangent, blocks, loss_mask, wi_gate, wi_up, wo_weight):
    row_count = hidden.shape[2]
    micro_count = hidden.shape[1]
    position = lax.iota(jnp.int32, row_count)
    offset = position % TLEN
    sequence = position // TLEN
    picker = (sequence[None, :] == lax.iota(jnp.int32, blocks.shape[2])[:, None]).astype(jnp.int32)
    limit_pos = jnp.sum(blocks[0][:, :, None] * picker[None, :, :], axis=1) * BLOCK
    weight = (offset[None, :] < limit_pos).astype(jnp.int32) * loss_mask[0]
    token_total = lax.psum(jnp.sum(weight), "dp")
    denominator = jnp.maximum(token_total, 1).astype(jnp.float32)
    states = hidden[0].astype(jnp.float32)
    squares = lax.psum(jnp.sum(states * states, axis=-1), "mp")
    normed = (states * lax.rsqrt(squares / D + 1e-06)[:, :, None] * gain).astype(jnp.bfloat16)
    tangent = cotangent[0] * weight[:, :, None].astype(jnp.bfloat16)
    zeros_grad = jnp.zeros((3, wi_gate.shape[0], wi_gate.shape[1]), jnp.float32)
    running_sum = zeros_grad
    compensation = zeros_grad
    for micro_step in range(micro_count):
        whole_normed, whole_tangent = (
            lax.all_gather(normed[micro_step], "mp", axis=1, tiled=True),
            lax.all_gather(tangent[micro_step], "mp", axis=1, tiled=True),
        )
        contrib = contributions(whole_normed, whole_tangent, wi_gate, wi_up, wo_weight)
        adjusted = contrib - compensation
        running = running_sum + adjusted
        compensation = running - running_sum - adjusted
        running_sum = running
    share_part = lax.psum_scatter(running_sum, "dp", scatter_dimension=2, tiled=True)
    share_part = share_part / denominator
    result = lax.all_gather(share_part, "dp", axis=2, tiled=True)
    return result


def solution(mesh):
    return jax.shard_map(
        on_device,
        mesh=mesh,
        in_specs=(
            P("dp", None, None, "mp"),
            P("mp"),
            P("dp", None, None, "mp"),
            P("dp", None, None),
            P("dp", None, None),
            P("mp", None),
            P("mp", None),
            P("mp", None),
        ),
        out_specs=P(None, "mp", None),
        check_vma=False,
    )
```

profile of v0, /device:TPU:0, one launch (start us, length us, event | category | flops | bytes accessed | tf_op | source)
XLA Modules:
  0.0 715.8 jit_solution(7229344962575830412)
XLA Ops:
  8.3 23.4 %psum.14 = f32[4,512]{1,0:T(4,128)S(1)} all-reduce(f32[4,512]{1,0:T(4,128)S(1)} %fusion.1), channel_id=1, replica_groups=mesh['dp'=4,'mp'=8] {'mp'}, use_global_device_ids=true, to_apply=%region_2.3 | all-reduce | flops 2048 | bytes 16384 | tf_op jit(solution)/shard_map/psum | solution.py:43
  42.0 40.1 %all-gather.26.cloned.1.call-done = bf16[1,512,2048]{2,1,0:T(8,128)(2,1)} async-done(((bf16[1,512,256]{2,1,0:T(8,128)(2,1)}), bf16[1,512,2048]{2,1,0:T(8,128)(2,1)}) %all-gather.26.cloned.1.call-update) | async-done | bytes 2097168 | tf_op jit(solution)/shard_map/all_gather | solution.py:51
  86.5 46.1 %all-gather.30.cloned.1.call-done = bf16[1,512,2048]{2,1,0:T(8,128)(2,1)} async-done(((bf16[1,512,256]{2,1,0:T(8,128)(2,1)}), bf16[1,512,2048]{2,1,0:T(8,128)(2,1)}) %all-gather.30.cloned.1.call-update) | async-done | bytes 2097168 | tf_op jit(solution)/shard_map/all_gather | solution.py:51
  132.7 4.6 fusion.15
  143.2 40.1 %all-gather.34.cloned.1.call-done = bf16[1,512,2048]{2,1,0:T(8,128)(2,1)} async-done(((bf16[1,512,256]{2,1,0:T(8,128)(2,1)}), bf16[1,512,2048]{2,1,0:T(8,128)(2,1)}) %all-gather.34.cloned.1.call-update) | async-done | bytes 2097168 | tf_op jit(solution)/shard_map/all_gather | solution.py:51
  183.3 4.6 fusion.6
  190.8 42.9 %all-gather.24.cloned.1.call-done = bf16[1,512,2048]{2,1,0:T(8,128)(2,1)} async-done(((bf16[1,512,256]{2,1,0:T(8,128)(2,1)}), bf16[1,512,2048]{2,1,0:T(8,128)(2,1)}) %all-gather.24.cloned.1.call-update) | async-done | bytes 2097168 | tf_op jit(solution)/shard_map/all_gather | solution.py:52
  233.7 5.3 fusion.29
  239.0 45.2 %all-gather.28.cloned.1.call-done = bf16[1,512,2048]{2,1,0:T(8,128)(2,1)} async-done(((bf16[1,512,256]{2,1,0:T(8,128)(2,1)}), bf16[1,512,2048]{2,1,0:T(8,128)(2,1)}) %all-gather.28.cloned.1.call-update) | async-done | bytes 2097168 | tf_op jit(solution)/shard_map/all_gather | solution.py:52
  305.3 29.3 %all-gather.32.cloned.1.call-done = bf16[1,512,2048]{2,1,0:T(8,128)(2,1)} async-done(((bf16[1,512,256]{2,1,0:T(8,128)(2,1)}), bf16[1,512,2048]{2,1,0:T(8,128)(2,1)}) %all-gather.32.cloned.1.call-update) | async-done | bytes 2097168 | tf_op jit(solution)/shard_map/all_gather | solution.py:52
  334.7 6.5 convolution_bitcast_fusion
  348.2 37.1 %all-gather.22.cloned.1.call-done = bf16[1,512,2048]{2,1,0:T(8,128)(2,1)} async-done(((bf16[1,512,256]{2,1,0:T(8,128)(2,1)}), bf16[1,512,2048]{2,1,0:T(8,128)(2,1)}) %all-gather.22.cloned.1.call-update) | async-done | bytes 2097168 | tf_op jit(solution)/shard_map/all_gather | solution.py:51
  385.3 4.6 fusion.33
  393.1 4.6 convolution_bitcast_fusion.8
  397.7 4.7 convolution_bitcast_fusion.5
  402.4 4.6 convolution_bitcast_fusion.2
  407.0 28.9 %all-gather.20.cloned.1.call-done = bf16[1,512,2048]{2,1,0:T(8,128)(2,1)} async-done(((bf16[1,512,256]{2,1,0:T(8,128)(2,1)}), bf16[1,512,2048]{2,1,0:T(8,128)(2,1)}) %all-gather.20.cloned.1.call-update) | async-done | bytes 2097168 | tf_op jit(solution)/shard_map/all_gather | solution.py:52
  444.7 5.2 convolution_bitcast_fusion.11
  454.0 20.6 %fusion = f32[3,640,2048]{2,1,0:T(8,128)} fusion(f32[1,640,2048]{2,1,0:T(8,128)} %convolution_bitcast_fusion, f32[1,640,2048]{2,1,0:T(8,128)} %convolution_bitcast_fusion.1, f32[1,640,2048]{2,1,0:T(8,128)} %convolution_bitcast_fusion.2, f32[1,640,2048]{2,1,0:T(8,128)S(1)} %bitcast.110, f32[1,640,2048]{2,1,0:T(8,128)S(1)} %bitcast.112, ...), kind=kLoop, calls=%fused_computation.4 | loop fusion | flops 74711040 | bytes 78643200 | tf_op jit(solution)/shard_map/add | solution.py:56
  474.7 5.5 psum.15
  480.8 108.7 %reduce-scatter.2.cloned.1.call-done = f32[3,640,512]{2,1,0:T(8,128)} async-done(((f32[3,640,2048]{2,1,0:T(8,128)}), f32[3,640,512]{2,1,0:T(8,128)}) %reduce-scatter.2.cloned.1.call-update) | async-done | bytes 3932176 | tf_op jit(solution)/shard_map/reduce_scatter | solution.py:59
  589.5 4.6 broadcast_divide_fusion
  594.2 100.1 %all-gather.18.cloned.1.call-done = f32[3,640,2048]{2,1,0:T(8,128)} async-done(((f32[3,640,512]{2,1,0:T(8,128)}), f32[3,640,2048]{2,1,0:T(8,128)}) %all-gather.18.cloned.1.call-update) | async-done | bytes 15728656 | tf_op jit(solution)/shard_map/all_gather | solution.py:61
  694.3 14.4 %copy.11 = f32[3,640,2048]{2,1,0:T(8,128)} copy(f32[3,640,2048]{2,1,0:T(8,128)} %all-gather.18.cloned.1.call-done) | data formatting | bytes 31457280
  (150 shorter events, 69.2 us)
Async XLA Ops:
  6.5 75.5 %copy-start = (bf16[640,2048]{1,0:T(8,128)(2,1)S(1)}, bf16[640,2048]{1,0:T(8,128)(2,1)}, u32[]{:S(2)}) copy-start(bf16[640,2048]{1,0:T(8,128)(2,1)} %param.13) | copy-start | bytes 7864324
  6.5 75.5 %all-gather.26.cloned.1.call-start = ((), (), s32[]{:S(2)}) async-start(), calls=%async_computation.6 | async-start | bytes 2359296 | tf_op jit(solution)/shard_map/all_gather | solution.py:51
  34.3 98.4 %all-gather.30.cloned.1.call-start = ((), (), s32[]{:S(2)}) async-start(), calls=%async_computation.8 | async-start | bytes 2359296 | tf_op jit(solution)/shard_map/all_gather | solution.py:51
  35.1 148.2 %all-gather.34.cloned.1.call-start = ((), (), s32[]{:S(2)}) async-start(), calls=%async_computation.10 | async-start | bytes 2359296 | tf_op jit(solution)/shard_map/all_gather | solution.py:51
  35.8 197.9 %all-gather.24.cloned.1.call-start = ((), (), s32[]{:S(2)}) async-start(), calls=%async_computation.5 | async-start | bytes 2359296 | tf_op jit(solution)/shard_map/all_gather | solution.py:52
  39.3 244.9 %all-gather.28.cloned.1.call-start = ((), (), s32[]{:S(2)}) async-start(), calls=%async_computation.7 | async-start | bytes 2359296 | tf_op jit(solution)/shard_map/all_gather | solution.py:52
  39.8 294.8 %all-gather.32.cloned.1.call-start = ((), (), s32[]{:S(2)}) async-start(), calls=%async_computation.9 | async-start | bytes 2359296 | tf_op jit(solution)/shard_map/all_gather | solution.py:52
  40.4 344.8 %all-gather.22.cloned.1.call-start = ((), (), s32[]{:S(2)}) async-start(), calls=%async_computation.4 | async-start | bytes 2359296 | tf_op jit(solution)/shard_map/all_gather | solution.py:51
  41.2 394.7 %all-gather.20.cloned.1.call-start = ((), (), s32[]{:S(2)}) async-start(), calls=%async_computation.3 | async-start | bytes 2359296 | tf_op jit(solution)/shard_map/all_gather | solution.py:52
  41.9 547.6 %reduce-scatter.2.cloned.1.call-start = ((), (), s32[]{:S(2)}) async-start(), calls=%async_computation.1 | async-start | bytes 19660800 | tf_op jit(solution)/shard_map/reduce_scatter | solution.py:59
  288.6 12.7 %copy-start.31 = (f32[512,640]{1,0:T(8,128)}, f32[512,640]{1,0:T(8,128)S(1)}, u32[]{:S(2)}) copy-start(f32[512,640]{1,0:T(8,128)S(1)} %fusion.20) | copy-start | bytes 3932164
  407.0 33.2 %copy-start.8 = (f32[512,640]{1,0:T(8,128)S(1)}, f32[512,640]{1,0:T(8,128)}, u32[]{:S(2)}) copy-start(f32[512,640]{1,0:T(8,128)} %fusion.33) | copy-start | bytes 3932164
  407.0 33.2 %copy-start.33 = (f32[512,640]{1,0:T(8,128)S(1)}, f32[512,640]{1,0:T(8,128)}, u32[]{:S(2)}) copy-start(f32[512,640]{1,0:T(8,128)} %fusion.35) | copy-start | bytes 3932164
  435.9 8.8 %copy-start.19 = (bf16[1,512,2048]{2,1,0:T(8,128)(2,1)S(1)}, bf16[1,512,2048]{2,1,0:T(8,128)(2,1)}, u32[]{:S(2)}) copy-start(bf16[1,512,2048]{2,1,0:T(8,128)(2,1)} %all-gather.22.cloned.1.call-done) | copy-start | bytes 6291460
  440.3 13.6 %slice-start = ((s8[5242880]{0:T(1024)(128)(4,1)}), s8[4194304]{0:T(1024)(128)(4,1)S(1)}, s32[]{:S(2)}) async-start(s8[5242880]{0:T(1024)(128)(4,1)} %bitcast.105), calls=%async_computation.11 | async-start | bytes 8388608
  440.3 13.6 %slice-start.2 = ((s8[5242880]{0:T(1024)(128)(4,1)}), s8[4194304]{0:T(1024)(128)(4,1)S(1)}, s32[]{:S(2)}) async-start(s8[5242880]{0:T(1024)(128)(4,1)} %bitcast.107), calls=%async_computation.13 | async-start | bytes 8388608
  440.3 13.6 %slice-start.4 = ((s8[5242880]{0:T(1024)(128)(4,1)}), s8[4194304]{0:T(1024)(128)(4,1)S(1)}, s32[]{:S(2)}) async-start(s8[5242880]{0:T(1024)(128)(4,1)} %bitcast.109), calls=%async_computation.15 | async-start | bytes 8388608
  440.3 13.6 %slice-start.6 = ((s8[5242880]{0:T(1024)(128)(4,1)}), s8[4194304]{0:T(1024)(128)(4,1)S(1)}, s32[]{:S(2)}) async-start(s8[5242880]{0:T(1024)(128)(4,1)} %bitcast.111), calls=%async_computation.17 | async-start | bytes 8388608
  444.7 9.2 %slice-start.1 = ((s8[5242880]{0:T(1024)(128)(4,1)}), s8[1048576]{0:T(1024)(128)(4,1)S(1)}, s32[]{:S(2)}) async-start(s8[5242880]{0:T(1024)(128)(4,1)} %bitcast.105), calls=%async_computation.12 | async-start | bytes 2097152
  444.7 9.2 %slice-start.3 = ((s8[5242880]{0:T(1024)(128)(4,1)}), s8[1048576]{0:T(1024)(128)(4,1)S(1)}, s32[]{:S(2)}) async-start(s8[5242880]{0:T(1024)(128)(4,1)} %bitcast.107), calls=%async_computation.14 | async-start | bytes 2097152
  444.7 9.2 %slice-start.5 = ((s8[5242880]{0:T(1024)(128)(4,1)}), s8[1048576]{0:T(1024)(128)(4,1)S(1)}, s32[]{:S(2)}) async-start(s8[5242880]{0:T(1024)(128)(4,1)} %bitcast.109), calls=%async_computation.16 | async-start | bytes 2097152
  444.7 9.2 %slice-start.7 = ((s8[5242880]{0:T(1024)(128)(4,1)}), s8[1048576]{0:T(1024)(128)(4,1)S(1)}, s32[]{:S(2)}) async-start(s8[5242880]{0:T(1024)(128)(4,1)} %bitcast.111), calls=%async_computation.18 | async-start | bytes 2097152
  474.6 219.6 %all-gather.18.cloned.1.call-start = ((), (), s32[]{:S(2)}) async-start(), calls=%async_computation.2 | async-start | bytes 19660800 | tf_op jit(solution)/shard_map/all_gather | solution.py:61
  694.3 14.4 %copy-start.1 = (bf16[640,2048]{1,0:T(8,128)(2,1)S(1)}, bf16[640,2048]{1,0:T(8,128)(2,1)}, u32[]{:S(2)}) copy-start(bf16[640,2048]{1,0:T(8,128)(2,1)} %param.13) | copy-start | bytes 7864324
  (36 other events, 148.9 us)
Sparse Core Ops, SparseCore 0:
  34.4 47.5 all-gather.25
  84.1 48.5 all-gather.29
  134.7 48.5 all-gather.33
  185.2 48.5 all-gather.23
  235.6 48.5 all-gather.27
  286.1 48.5 all-gather.31
  336.7 48.5 all-gather.21
  387.3 48.5 all-gather.19
  474.7 114.7 reduce-scatter.1
  594.3 99.9 all-gather.17
where the time goes:
time: 726 us; the launch traced here: 716 us
  waiting for transfers between devices  522 us (72%)
  matrix products  101 us (14%)
  other arithmetic  30.9 us (4%)
  blocking collectives  28.9 us (4%)
  local copies, waits for them, and re-layouts  17.7 us (2%)
  between operations  14.9 us (2%)
    all_gather x4, waiting for transfers between devices, on_device(): lax.all_gather(normed[micro_step], 'mp', axis=1, tiled=True)  163 us
    all_gather x4, waiting for transfers between devices, on_device(): lax.all_gather(tangent[micro_step], 'mp', axis=1, tiled=True)  146 us
    reduce_scatter x1, waiting for transfers between devices, on_device(): lax.psum_scatter(running_sum, 'dp', scatter_dimension=2, tiled=True)  109 us
    all_gather x1, waiting for transfers between devices, on_device(): result = lax.all_gather(share_part, 'dp', axis=2, tiled=True)  100 us
    psum x1, blocking collectives, on_device(): squares = lax.psum(jnp.sum(states * states, axis=-1), 'mp')  23.4 us
    add x1, other arithmetic, on_device(): running = running_sum + adjusted  20.6 us
    dot_general x4, matrix products, contributions(): lax.dot_general(inner, tangent, dims, preferred_element_type=jnp.float32)  19.5 us
    dot_general x4, matrix products, contributions(): lax.dot_general(grad_gate, normed, dims, preferred_element_type=jnp.float32)  19 us
  transfers between devices with their start and end apart: 10, of which 10 were waited for; matrix products, arithmetic and copies ran while one was open for 12% of the time, Pallas kernels for 0%

commit v1 on v0

v1 whole, which is shorter than its diff:
```python
import functools

import jax
import jax.numpy as jnp
from jax import lax
from jax.experimental import pallas as pl
from jax.experimental.pallas import tpu as pltpu
from jax.sharding import PartitionSpec as P

BLOCK = 128
TLEN = 256
MESH = pl.DeviceIdType.MESH


def ring_index(place, n):
    back = place // (n // 2)
    return (1 - back) * (2 * place) + back * (2 * (n - 1 - place) + 1)


def ring_place(index, n):
    odd = index % 2
    return (1 - odd) * (index // 2) + odd * (n - 1 - index // 2)


def gather_kernel(n, wide, h_ref, t_ref, hg_ref, tg_ref, local_sem, send_sem, recv_sem):
    micro, rows, cols = h_ref.shape
    me = lax.axis_index("mp")
    place = ring_place(me, n)
    ahead = ring_index(lax.rem(place + 1, n), n)
    behind = ring_index(lax.rem(place + n - 1, n), n)

    def spot(ref, owner, m):
        if wide:
            return ref.at[m, :, pl.ds(pl.multiple_of(owner * cols, cols), cols)]
        return ref.at[owner, m]

    barrier = pltpu.get_barrier_semaphore()
    for peer in (ahead, behind):
        pl.semaphore_signal(barrier, inc=1, device_id={"mp": peer}, device_id_type=MESH)
    pl.semaphore_wait(barrier, 2)

    own = []
    copies = {}
    for step in range(n - 1):
        for m in range(micro):
            for way, (src, dst, peer, sign) in enumerate(((h_ref, hg_ref, ahead, -1), (t_ref, tg_ref, behind, 1))):
                owner = ring_index(lax.rem(place + sign * step + n, n), n)
                if step > 0:
                    copies[step - 1, m, way].wait_recv()
                copy = pltpu.make_async_remote_copy(
                    src_ref=src.at[m] if step == 0 else spot(dst, owner, m),
                    dst_ref=spot(dst, owner, m),
                    send_sem=send_sem.at[way, step, m],
                    recv_sem=recv_sem.at[way, step, m],
                    device_id={"mp": peer},
                    device_id_type=MESH,
                )
                copy.start()
                copies[step, m, way] = copy
        if step == 0:
            for m in range(micro):
                for way, (src, dst) in enumerate(((h_ref, hg_ref), (t_ref, tg_ref))):
                    keep = pltpu.make_async_copy(src.at[m], spot(dst, me, m), local_sem.at[way, m])
                    keep.start()
                    own.append(keep)
    for (step, m, way), copy in copies.items():
        copy.wait_send()
        if step == n - 2:
            copy.wait_recv()
    for keep in own:
        keep.wait()


def gather_rows(hidden, tangent, n):
    micro, rows, cols = hidden.shape
    wide = cols % 128 == 0
    shape = (micro, rows, n * cols) if wide else (n, micro, rows, cols)
    hg, tg = pl.pallas_call(
        functools.partial(gather_kernel, n, wide),
        out_shape=[jax.ShapeDtypeStruct(shape, hidden.dtype)] * 2,
        in_specs=[pl.BlockSpec(memory_space=pl.ANY)] * 2,
        out_specs=[pl.BlockSpec(memory_space=pl.ANY)] * 2,
        scratch_shapes=[
            pltpu.SemaphoreType.DMA((2, micro)),
            pltpu.SemaphoreType.DMA((2, n - 1, micro)),
            pltpu.SemaphoreType.DMA((2, n - 1, micro)),
        ],
        compiler_params=pltpu.CompilerParams(collective_id=0, has_side_effects=True),
        name="gather_rows",
    )(hidden, tangent)
    if not wide:
        hg, tg = (jnp.transpose(a, (1, 2, 0, 3)).reshape(micro, rows, n * cols) for a in (hg, tg))
    return hg, tg


def gelu_tanh(value):
    return jax.nn.gelu(value, approximate=True)


def factors(normed, tangent, wi_gate, wi_up, wo_weight):
    rows_dims = (((1,), (1,)), ((), ()))
    gate_pre = lax.dot_general(normed, wi_gate, rows_dims, preferred_element_type=jnp.float32)
    up_pre = lax.dot_general(normed, wi_up, rows_dims, preferred_element_type=jnp.float32)
    activated, pullback = jax.vjp(gelu_tanh, gate_pre)
    inner = (activated * up_pre).astype(jnp.bfloat16)
    back_grad = lax.dot_general(tangent, wo_weight, rows_dims, preferred_element_type=jnp.float32)
    grad_gate = pullback(back_grad * up_pre)[0].astype(jnp.bfloat16)
    grad_up = (back_grad * activated).astype(jnp.bfloat16)
    return grad_gate, grad_up, inner


def kahan(pairs):
    dims = (((0,), (0,)), ((), ()))
    total = comp = None
    for left, right in pairs:
        term = lax.dot_general(left, right, dims, preferred_element_type=jnp.float32)
        if total is None:
            total, comp = term, jnp.zeros_like(term)
            continue
        adjusted = term - comp
        running = total + adjusted
        comp = running - total - adjusted
        total = running
    return total


def swap(value, bit, size):
    return lax.ppermute(value, "dp", [(i, i ^ bit) for i in range(size)])


def reduce_groups(total, denominator, size):
    core = lax.axis_index("dp") % 2
    half = total.shape[1] // 2
    give = lax.dynamic_slice_in_dim(total, (1 - core) * half, half, 1).astype(jnp.bfloat16)
    keep = lax.dynamic_slice_in_dim(total, core * half, half, 1)
    part = keep + swap(give, 1, size).astype(jnp.float32)
    bit = 2
    while bit < size:
        mine = part.astype(jnp.bfloat16)
        part = mine.astype(jnp.float32) + swap(mine, bit, size).astype(jnp.float32)
        bit *= 2
    mine = (part / denominator).astype(jnp.bfloat16)
    theirs = swap(mine, 1, size)
    low = jnp.where(core == 0, mine, theirs)
    high = jnp.where(core == 0, theirs, mine)
    return jnp.concatenate([low, high], axis=1).astype(jnp.float32)


def on_device(n, groups, hidden, gain, cotangent, blocks, loss_mask, wi_gate, wi_up, wo_weight):
    row_count = hidden.shape[2]
    micro_count = hidden.shape[1]
    position = lax.iota(jnp.int32, row_count)
    offset = position % TLEN
    sequence = position // TLEN
    picker = (sequence[None, :] == lax.iota(jnp.int32, blocks.shape[2])[:, None]).astype(jnp.int32)
    limit_pos = jnp.sum(blocks[0][:, :, None] * picker[None, :, :], axis=1) * BLOCK
    weight = (offset[None, :] < limit_pos).astype(jnp.int32) * loss_mask[0]
    token_total = lax.psum(jnp.sum(weight), "dp")
    denominator = jnp.maximum(token_total, 1).astype(jnp.float32)
    whole_gain = lax.all_gather(gain, "mp", axis=0, tiled=True)
    tangent = cotangent[0] * weight[:, :, None].astype(jnp.bfloat16)
    states, whole_tangent = gather_rows(hidden[0], tangent, n)
    states = states.astype(jnp.float32)
    squares = jnp.mean(states * states, axis=-1, keepdims=True)
    normed = (states * lax.rsqrt(squares + 1e-06) * whole_gain).astype(jnp.bfloat16)
    made = [factors(normed[m], whole_tangent[m], wi_gate, wi_up, wo_weight) for m in range(micro_count)]
    results = []
    for which in (2, 1, 0):
        right = whole_tangent if which == 2 else normed
        total = kahan([(made[m][which], right[m]) for m in range(micro_count)])
        results.append(reduce_groups(total, denominator, groups))
    return jnp.stack(results[::-1])


def solution(mesh):
    return jax.shard_map(
        functools.partial(on_device, mesh.shape["mp"], mesh.shape["dp"]),
        mesh=mesh,
        in_specs=(
            P("dp", None, None, "mp"),
            P("mp"),
            P("dp", None, None, "mp"),
            P("dp", None, None),
            P("dp", None, None),
            P("mp", None),
            P("mp", None),
            P("mp", None),
        ),
        out_specs=P(None, "mp", None),
        check_vma=False,
    )
```

time: 726 us -> 413 us (0.57)
  waiting for transfers between devices: 522 us -> 0.02 us
  Pallas kernels: 0 us -> 164 us
  blocking collectives: 28.9 us -> 99 us
  matrix products: 101 us -> 86.1 us
  other arithmetic: 30.9 us -> 45.1 us
  between operations: 14.9 us -> 1.45 us
  local copies, waits for them, and re-layouts: 17.7 us -> 9.77 us
    all_gather x9 -> x0, waiting for transfers between devices: 410 us -> none  [the longest x4 163 us: on_device(): lax.all_gather(normed[micro_step], 'mp', axis=1, tiled=True)]
    pallas_call x0 -> x1, Pallas kernels: none -> 164 us  [gather_rows(): pl.pallas_call(functools.partial(gather_kernel, n, wide), out_shape=[jax....]
    reduce_scatter x1 -> x0, waiting for transfers between devices: 109 us -> none  [on_device(): lax.psum_scatter(running_sum, 'dp', scatter_dimension=2, tiled=True)]
    psum x1, blocking collectives: 5.48 us -> 78.8 us  [on_device(): token_total = lax.psum(jnp.sum(weight), 'dp')]
    psum x1 -> x0, blocking collectives: 23.4 us -> none  [on_device(): squares = lax.psum(jnp.sum(states * states, axis=-1), 'mp')]
    convert_element_type x1 -> x7, other arithmetic: 1.57 us -> 24.1 us  [the longest x1 8.79 us: on_device(): (states * lax.rsqrt(squares + 1e-06) * whole_gain).astype(jnp.bfloat16)]
    add x1 -> x0, other arithmetic: 20.6 us -> none  [on_device(): running = running_sum + adjusted]
    all_gather x0 -> x1, blocking collectives: none -> 20.2 us  [on_device(): whole_gain = lax.all_gather(gain, 'mp', axis=0, tiled=True)]
  transfers between devices with their start and end apart: 10 -> 9, of which waited for: 10 -> 0; matrix products, arithmetic and copies ran while one was open for 12% -> 12% of each run, Pallas kernels for 0% -> 0%
where the time goes in v1:
time: 413 us; the launch traced here: 410 us
  Pallas kernels  164 us (40%)
  blocking collectives  99 us (24%)
  matrix products  86.1 us (21%)
  other arithmetic  45.1 us (11%)
  local copies, waits for them, and re-layouts  9.77 us (2%)
  starting transfers between devices  4.53 us (1%)
    pallas_call x1, Pallas kernels, gather_rows(): pl.pallas_call(functools.partial(gather_kernel, n, wide), out_shape=[jax....  164 us
    psum x1, blocking collectives, on_device(): token_total = lax.psum(jnp.sum(weight), 'dp')  78.8 us
    dot_general x12, matrix products, kahan(): lax.dot_general(left, right, dims, preferred_element_type=jnp.float32)  49.1 us
    all_gather x1, blocking collectives, on_device(): whole_gain = lax.all_gather(gain, 'mp', axis=0, tiled=True)  20.2 us
    dot_general x4, matrix products, factors(): lax.dot_general(normed, wi_gate, rows_dims, preferred_element_type=jnp.fl...  13.7 us
    dot_general x4, matrix products, factors(): lax.dot_general(tangent, wo_weight, rows_dims, preferred_element_type=jnp...  11.6 us
    dot_general x4, matrix products, factors(): lax.dot_general(normed, wi_up, rows_dims, preferred_element_type=jnp.floa...  11.6 us
    convert_element_type x1, other arithmetic, on_device(): (states * lax.rsqrt(squares + 1e-06) * whole_gain).astype(jnp.bfloat16)  8.79 us
  transfers between devices with their start and end apart: 9, of which 0 were waited for; matrix products, arithmetic and copies ran while one was open for 12% of the time, Pallas kernels for 0%

profile of v1, /device:TPU:0, one launch (start us, length us, event | category | flops | bytes accessed | tf_op | source)
XLA Modules:
  0.0 409.7 jit_solution(16481609354995289802)
XLA Ops:
  4.8 163.7 %gather_rows.1 = (bf16[4,512,2048]{2,1,0:T(8,128)(2,1)}, bf16[4,512,2048]{2,1,0:T(8,128)(2,1)}) custom-call(bf16[4,512,256]{2,1,0:T(8,128)(2,1)} %bitcast.86, bf16[4,512,256]{2,1,0:T(8,128)(2,1)} %bitcast_multiply_fusion.t_ref), custom_call_target="tpu_custom_call" | custom-call | tf_op jit(solution)/shard_map/gather_rows/pallas_call | solution.py:78
  168.6 5.1 %fusion = f32[4,512]{1,0:T(4,128)S(1)} fusion(bf16[4,512,2048]{2,1,0:T(8,128)(2,1)} %get-tuple-element.8), kind=kLoop, calls=%fused_computation.2 | loop fusion | flops 12580864 | bytes 8396800 | tf_op jit(solution)/shard_map/reduce_sum | solution.py:164
  173.7 20.2 %all-gather = f32[8,1,256]{2,1,0:T(1,128)S(1)} all-gather(f32[1,1,256]{2,1,0:T(1,128)S(1)} %bitcast.88), channel_id=1, replica_groups=mesh['dp'=4,'mp'=8] {'mp'}, dimensions={0}, use_global_device_ids=true | all-gather | bytes 9216 | tf_op jit(solution)/shard_map/all_gather | solution.py:160
  193.9 8.8 %fusion.2 = bf16[4,512,2048]{2,1,0:T(8,128)(2,1)} fusion(bf16[4,512,2048]{2,1,0:T(8,128)(2,1)} %get-tuple-element.8, f32[2048]{0:T(1024)S(1)} %bitcast.87, f32[4,512]{1,0:T(4,128)S(1)} %add_rsqrt_fusion), kind=kLoop, calls=%fused_computation.4 | loop fusion | flops 16777216 | bytes 16793600 | tf_op jit(solution)/shard_map/convert_element_type | solution.py:165
  202.7 4.6 %fusion.28 = f32[512,640]{1,0:T(8,128)} fusion(bf16[640,2048]{1,0:T(8,128)(2,1)S(1)} %copy-done, bf16[4,512,2048]{2,1,0:T(8,128)(2,1)} %fusion.2), kind=kOutput, calls=%fused_computation.55 | convolution fusion | flops 1342177280 | bytes 6029312 | tf_op jit(solution)/shard_map/dot_general | solution.py:102
  207.3 3.0 fusion.32
  216.6 2.9 fusion.16
  222.4 3.1 fusion.36
  225.6 2.9 fusion.37
  228.5 2.9 fusion.8
  231.4 3.0 fusion.38
  240.2 4.8 %fusion.27 = f32[640,2048]{1,0:T(8,128)S(1)} fusion(bf16[4,512,2048]{2,1,0:T(8,128)(2,1)} %fusion.2, f32[512,640]{1,0:T(8,128)S(1)} %copy-done.4, f32[512,640]{1,0:T(8,128)} %fusion.16, f32[512,640]{1,0:T(8,128)} %fusion.29), kind=kOutput, calls=%fused_computation.54 | convolution fusion | flops 1349058560 | bytes 11272192 | tf_op jit(solution)/shard_map/dot_general | solution.py:116
  245.0 6.3 %fusion.31 = f32[640,2048]{1,0:T(8,128)} fusion(bf16[4,512,2048]{2,1,0:T(8,128)(2,1)} %fusion.2, f32[512,640]{1,0:T(8,128)S(1)} %copy-done.3, f32[512,640]{1,0:T(8,128)S(1)} %copy-done.15, f32[512,640]{1,0:T(8,128)S(1)} %copy-done.10), kind=kOutput, calls=%fused_computation.58 | convolution fusion | flops 1349058560 | bytes 11272192 | tf_op jit(solution)/shard_map/dot_general | solution.py:116
  251.4 6.6 %fusion.35 = f32[640,2048]{1,0:T(8,128)} fusion(bf16[4,512,2048]{2,1,0:T(8,128)(2,1)} %fusion.2, f32[512,640]{1,0:T(8,128)S(1)} %copy-done.5, f32[512,640]{1,0:T(8,128)S(1)} %copy-done.17, f32[512,640]{1,0:T(8,128)S(1)} %copy-done.13), kind=kOutput, calls=%fused_computation.62 | convolution fusion | flops 1349058560 | bytes 11272192 | tf_op jit(solution)/shard_map/dot_general | solution.py:116
  258.0 6.6 %subtract_add_fusion.2 = f32[640,2048]{1,0:T(8,128)S(1)} fusion(f32[640,2048]{1,0:T(8,128)} %fusion.35, f32[640,2048]{1,0:T(8,128)} %fusion.31, f32[640,2048]{1,0:T(8,128)S(1)} %fusion.27, bf16[4,512,2048]{2,1,0:T(8,128)(2,1)S(1)} %bitcast.81, f32[512,640]{1,0:T(8,128)S(1)} %copy-done.22, f32[512,640]{1,0:T(8,128)S(1)} %copy-done.27, ...), kind=kOutput, calls=%fused_computation.8 | convolution fusion | flops 1360855040 | bytes 27000832 | tf_op jit(solution)/shard_map/dot_general | solution.py:116
  272.6 6.2 %subtract_add_fusion.1 = f32[640,2048]{1,0:T(8,128)} fusion(f32[640,2048]{1,0:T(8,128)S(1)} %fusion.34, f32[640,2048]{1,0:T(8,128)S(1)} %fusion.30, f32[640,2048]{1,0:T(8,128)S(1)} %fusion.26, bf16[4,512,2048]{2,1,0:T(8,128)(2,1)S(1)} %bitcast.81, f32[512,640]{1,0:T(8,128)} %fusion.4, f32[512,640]{1,0:T(8,128)S(1)} %copy-done.23), kind=kOutput, calls=%fused_computation.7 | convolution fusion | flops 1357250560 | bytes 25690112 | tf_op jit(solution)/shard_map/dot_general | solution.py:116
  278.8 3.1 dynamic-slice_convert_fusion.1
  282.5 3.5 fusion.14
  286.0 3.5 fusion.10
  291.4 4.7 %subtract_add_fusion = f32[640,2048]{1,0:T(8,128)} fusion(f32[640,2048]{1,0:T(8,128)S(1)} %fusion.6, f32[640,2048]{1,0:T(8,128)S(1)} %fusion.10, f32[640,2048]{1,0:T(8,128)S(1)} %fusion.14, bf16[4,512,2048]{2,1,0:T(8,128)(2,1)S(1)} %bitcast.85, f32[512,640]{1,0:T(8,128)S(1)} %copy-done.26, f32[512,640]{1,0:T(8,128)S(1)} %copy-done.24), kind=kOutput, calls=%fused_computation.6 | convolution fusion | flops 1357250560 | bytes 25690112 | tf_op jit(solution)/shard_map/dot_general | solution.py:116
  296.1 3.0 dynamic-slice_convert_fusion
  311.0 78.8 %psum.7 = s32[]{:T(128)} all-reduce(s32[]{:T(128)} %get-tuple-element.15), channel_id=1, replica_groups=mesh['dp'=4,'mp'=8] {'dp'}, use_global_device_ids=true, to_apply=%region_3.4 | all-reduce | flops 1 | bytes 8 | tf_op jit(solution)/shard_map/psum | solution.py:158
  390.3 3.0 divide_convert_fusion.2
  403.0 6.2 %maximum_convert_fusion = f32[3,640,2048]{2,1,0:T(8,128)} fusion(bf16[1,640,1024]{2,1,0:T(8,128)(2,1)S(1)} %get-tuple-element.14, bf16[1,640,1024]{2,1,0:T(8,128)(2,1)S(1)} %get-tuple-element.13, bf16[1,640,1024]{2,1,0:T(8,128)(2,1)S(1)} %get-tuple-element.12, bf16[1,640,1024]{2,1,0:T(8,128)(2,1)S(1)} %get-tuple-element.11, ...), kind=kLoop, calls=%fused_computation.5 | loop fusion | flops 47185920 | bytes 23592960 | tf_op jit(solution)/shard_map/stack | solution.py:172
  (113 shorter events, 51.7 us)
Async XLA Ops:
  0.0 202.7 %copy-start = (bf16[640,2048]{1,0:T(8,128)(2,1)S(1)}, bf16[640,2048]{1,0:T(8,128)(2,1)}, u32[]{:S(2)}) copy-start(bf16[640,2048]{1,0:T(8,128)(2,1)} %param.13) | copy-start | bytes 7864324
  168.6 5.1 %copy-start.19 = (f32[256]{0:T(256)S(1)}, f32[256]{0:T(256)}, u32[]{:S(2)}) copy-start(f32[256]{0:T(256)} %param.9) | copy-start | bytes 3076
  210.3 5.8 %slice-start.2 = ((s8[8388608]{0:T(1024)(128)(4,1)}), s8[4194304]{0:T(1024)(128)(4,1)S(1)}, s32[]{:S(2)}) async-start(s8[8388608]{0:T(1024)(128)(4,1)} %bitcast.82), calls=%async_computation.2 | async-start | bytes 8388608
  240.2 4.8 %copy-start.10 = (f32[512,640]{1,0:T(8,128)S(1)}, f32[512,640]{1,0:T(8,128)}, u32[]{:S(2)}) copy-start(f32[512,640]{1,0:T(8,128)} %fusion.33) | copy-start | bytes 3932164
  240.2 4.8 %copy-start.15 = (f32[512,640]{1,0:T(8,128)S(1)}, f32[512,640]{1,0:T(8,128)}, u32[]{:S(2)}) copy-start(f32[512,640]{1,0:T(8,128)} %fusion.12) | copy-start | bytes 3932164
  245.0 6.4 %copy-start.5 = (f32[512,640]{1,0:T(8,128)S(1)}, f32[512,640]{1,0:T(8,128)}, u32[]{:S(2)}) copy-start(f32[512,640]{1,0:T(8,128)} %fusion.36) | copy-start | bytes 3932164
  245.0 6.4 %copy-start.13 = (f32[512,640]{1,0:T(8,128)S(1)}, f32[512,640]{1,0:T(8,128)}, u32[]{:S(2)}) copy-start(f32[512,640]{1,0:T(8,128)} %fusion.37) | copy-start | bytes 3932164
  245.0 6.4 %copy-start.17 = (f32[512,640]{1,0:T(8,128)S(1)}, f32[512,640]{1,0:T(8,128)}, u32[]{:S(2)}) copy-start(f32[512,640]{1,0:T(8,128)} %fusion.8) | copy-start | bytes 3932164
  245.0 13.0 %slice-start = ((s8[8388608]{0:T(1024)(128)(4,1)}), s8[4194304]{0:T(1024)(128)(4,1)S(1)}, s32[]{:S(2)}) async-start(s8[8388608]{0:T(1024)(128)(4,1)} %bitcast.80), calls=%async_computation | async-start | bytes 8388608
  251.4 6.6 %slice-start.1 = ((s8[8388608]{0:T(1024)(128)(4,1)}), s8[4194304]{0:T(1024)(128)(4,1)S(1)}, s32[]{:S(2)}) async-start(s8[8388608]{0:T(1024)(128)(4,1)} %bitcast.80), calls=%async_computation.1 | async-start | bytes 8388608
  251.4 6.6 %copy-start.22 = (f32[512,640]{1,0:T(8,128)S(1)}, f32[512,640]{1,0:T(8,128)}, u32[]{:S(2)}) copy-start(f32[512,640]{1,0:T(8,128)} %fusion.38) | copy-start | bytes 3932164
  251.4 6.6 %copy-start.25 = (f32[512,640]{1,0:T(8,128)S(1)}, f32[512,640]{1,0:T(8,128)}, u32[]{:S(2)}) copy-start(f32[512,640]{1,0:T(8,128)} %fusion.39) | copy-start | bytes 3932164
  251.4 6.6 %copy-start.27 = (f32[512,640]{1,0:T(8,128)S(1)}, f32[512,640]{1,0:T(8,128)}, u32[]{:S(2)}) copy-start(f32[512,640]{1,0:T(8,128)} %fusion.4) | copy-start | bytes 3932164
  267.4 31.7 %collective-permute-start = (bf16[640,1024]{1,0:T(8,128)(2,1)}, bf16[640,1024]{1,0:T(8,128)(2,1)}, u32[]{:S(2)}, u32[]{:S(2)}) collective-permute-start(bf16[640,1024]{1,0:T(8,128)(2,1)} %dynamic-slice_convert_fusion.2), channel_id=1, source_target_pairs={{0,8},{8,0},{16,24},{24,16},{1,9},{9,1},{17,25},{25,17},{2,10},{10... | collective-permute-start | bytes 3932168 | tf_op jit(solution)/shard_map/ppermute | solution.py:128
  282.0 21.3 %collective-permute-start.3 = (bf16[640,1024]{1,0:T(8,128)(2,1)}, bf16[640,1024]{1,0:T(8,128)(2,1)}, u32[]{:S(2)}, u32[]{:S(2)}) collective-permute-start(bf16[640,1024]{1,0:T(8,128)(2,1)} %dynamic-slice_convert_fusion.1), channel_id=1, source_target_pairs={{0,8},{8,0},{16,24},{24,16},{1,9},{9,1},{17,25},{25,17},{2,10},{10... | collective-permute-start | bytes 3932168 | tf_op jit(solution)/shard_map/ppermute | solution.py:128
  282.5 7.1 %slice-start.4 = ((s8[8388608]{0:T(1024)(128)(4,1)}), s8[4194304]{0:T(1024)(128)(4,1)S(1)}, s32[]{:S(2)}) async-start(s8[8388608]{0:T(1024)(128)(4,1)} %bitcast.84), calls=%async_computation.4 | async-start | bytes 8388608
  299.1 7.5 %collective-permute-start.6 = (bf16[640,1024]{1,0:T(8,128)(2,1)}, bf16[640,1024]{1,0:T(8,128)(2,1)}, u32[]{:S(2)}, u32[]{:S(2)}) collective-permute-start(bf16[640,1024]{1,0:T(8,128)(2,1)} %dynamic-slice_convert_fusion), channel_id=1, source_target_pairs={{0,8},{8,0},{16,24},{24,16},{1,9},{9,1},{17,25},{25,17},{2,10},{10... | collective-permute-start | bytes 3932168 | tf_op jit(solution)/shard_map/ppermute | solution.py:128
  301.7 88.6 %collective-permute-start.1 = (bf16[640,1024]{1,0:T(8,128)(2,1)S(1)}, bf16[640,1024]{1,0:T(8,128)(2,1)}, u32[]{:S(2)}, u32[]{:S(2)}) collective-permute-start(bf16[640,1024]{1,0:T(8,128)(2,1)S(1)} %add_convert_fusion.2), channel_id=1, source_target_pairs={{0,16},{8,24},{16,0},{24,8},{1,17},{9,25},{17,1},{25,9},{2,18},{10... | collective-permute-start | bytes 3932168 | tf_op jit(solution)/shard_map/ppermute | solution.py:128
  306.0 87.3 %collective-permute-start.4 = (bf16[640,1024]{1,0:T(8,128)(2,1)S(1)}, bf16[640,1024]{1,0:T(8,128)(2,1)}, u32[]{:S(2)}, u32[]{:S(2)}) collective-permute-start(bf16[640,1024]{1,0:T(8,128)(2,1)S(1)} %add_convert_fusion.1), channel_id=1, source_target_pairs={{0,16},{8,24},{16,0},{24,8},{1,17},{9,25},{17,1},{25,9},{2,18},{10... | collective-permute-start | bytes 3932168 | tf_op jit(solution)/shard_map/ppermute | solution.py:128
  309.8 86.0 %collective-permute-start.7 = (bf16[640,1024]{1,0:T(8,128)(2,1)}, bf16[640,1024]{1,0:T(8,128)(2,1)}, u32[]{:S(2)}, u32[]{:S(2)}) collective-permute-start(bf16[640,1024]{1,0:T(8,128)(2,1)} %add_convert_fusion), channel_id=1, source_target_pairs={{0,16},{8,24},{16,0},{24,8},{1,17},{9,25},{17,1},{25,9},{2,18},{10... | collective-permute-start | bytes 3932168 | tf_op jit(solution)/shard_map/ppermute | solution.py:128
  393.3 4.8 %collective-permute-start.2 = (bf16[640,1024]{1,0:T(8,128)(2,1)}, bf16[640,1024]{1,0:T(8,128)(2,1)}, u32[]{:S(2)}, u32[]{:S(2)}) collective-permute-start(bf16[640,1024]{1,0:T(8,128)(2,1)} %divide_convert_fusion.2), channel_id=1, source_target_pairs={{0,8},{8,0},{16,24},{24,16},{1,9},{9,1},{17,25},{25,17},{2,10},{10... | collective-permute-start | bytes 3932168 | tf_op jit(solution)/shard_map/ppermute | solution.py:128
  395.2 4.8 %collective-permute-start.5 = (bf16[640,1024]{1,0:T(8,128)(2,1)S(1)}, bf16[640,1024]{1,0:T(8,128)(2,1)}, u32[]{:S(2)}, u32[]{:S(2)}) collective-permute-start(bf16[640,1024]{1,0:T(8,128)(2,1)S(1)} %divide_convert_fusion.1), channel_id=1, source_target_pairs={{0,8},{8,0},{16,24},{24,16},{1,9},{9,1},{17,25},{25,17},{2,10},{10... | collective-permute-start | bytes 3932168 | tf_op jit(solution)/shard_map/ppermute | solution.py:128
  398.0 3.5 collective-permute-start.8
  403.0 6.2 %copy-start.1 = (bf16[640,2048]{1,0:T(8,128)(2,1)S(1)}, bf16[640,2048]{1,0:T(8,128)(2,1)}, u32[]{:S(2)}) copy-start(bf16[640,2048]{1,0:T(8,128)(2,1)} %param.13) | copy-start | bytes 7864324
  (19 other events, 57.8 us)
